TPU v7x, 32 devices: a whole 2x2x4 slice. The times are simulated.
32 devices in a mesh: ctx: 4 (over z), head: 4 (over x, core), rep: 2 (over y).
Axes of the slice: x: 2, y: 2, z: 4, core: 2. Of those that a mesh axis runs over, the one named last changes fastest.
Arguments:
- queries: bfloat16 [4, 256, 2048], P('rep', 'ctx', 'head'), may hold values from -6 to 6
- keyvals: bfloat16 [4, 256, 4, 128], P('rep', 'ctx', 'head'), may hold values from -6 to 6
- sinks: float32 [32], P('head'), may hold values from -1 to 3
- stream: bfloat16 [4, 256, 2880], P('rep', 'ctx', 'head'), may hold values from -6 to 6
- out_weight: bfloat16 [2048, 2880], P('head', 'ctx'), may hold values from -0.75 to 0.75
- norm_gain: float32 [2880], replicated, may hold values from 0.1 to 1.9
- router: bfloat16 [2880, 32], replicated, may hold values from -0.12 to 0.12
- expert_ids: int32 [4, 256, 4], P('rep', 'ctx'), may hold values from 0 to 31, all different within a row; in each aligned block of 64 rows (0 to 63, 64 to 127, ..., all dimensions but the last counted through in order) at most 12 rows name the same one
- w_gate_up: bfloat16 [64, 720, 5760], P('ctx', 'head'), may hold values from -0.109375 to 0.109375
- w_down: bfloat16 [64, 720, 2880], P('ctx', None, 'head'), may hold values from -0.15625 to 0.15625
Outputs:
- layer_out: bfloat16 [4, 256, 2880], P('rep', 'ctx', 'head')
Inputs may be any that keep to these rules, and one draw needn't show every extreme that they name: `expert_ids`: each position names 4 different experts. Within each aligned block of 64 positions of a sequence no expert is named by more than 12 positions, and in every draw some block has an expert named by exactly 12.
All inputs are finite; a program needn't handle non-finite values.
Results may differ from a plain program's by a relative error of at most 0.015.
Values may be sent and summed in bfloat16 or wider, within the bound.
A program may use at most 192 MiB of HBM per device.

v0:
```python
import jax
import jax.numpy as jnp
from jax import lax
from jax.sharding import PartitionSpec as P


def on_device(
    queries, keyvals, sinks, stream, out_weight, norm_gain, router, expert_ids, w_gate_up, w_down
):
    ctx_count = lax.axis_size("ctx")
    rep_count = lax.axis_size("rep")
    local_seqs = queries.shape[0]
    tokens = queries.shape[1]
    row_count = local_seqs * tokens
    kv_local = keyvals.shape[2]
    head_dim = keyvals.shape[3] // 2
    q_local = queries.shape[2] // head_dim
    query_group_size = q_local // kv_local
    wide_rows = query_group_size * tokens
    col_width = stream.shape[2]
    first_pos = lax.axis_index("ctx") * tokens
    last_pos = first_pos + tokens - 1
    score_scale = head_dim ** (-0.5)
    scaled_queries = queries * jnp.asarray(score_scale, jnp.bfloat16)
    query_grid = scaled_queries.reshape(local_seqs, tokens, kv_local, query_group_size, head_dim)
    query_wide = jnp.transpose(query_grid, (0, 2, 3, 1, 4)).reshape(
        local_seqs, kv_local, wide_rows, head_dim
    )
    positions = first_pos + jnp.tile(jnp.arange(tokens), query_group_size)
    sink_rows = jnp.repeat(sinks.reshape(kv_local, query_group_size), tokens, axis=1)
    sink_grid = jnp.broadcast_to(sink_rows[None], (local_seqs, kv_local, wide_rows))
    start_state = (
        sink_grid,
        jnp.ones_like(sink_grid),
        jnp.zeros((local_seqs, kv_local, head_dim, wide_rows), jnp.float32),
    )
    gate_up_weights = w_gate_up.reshape(
        w_gate_up.shape[0], w_gate_up.shape[1], 2, w_gate_up.shape[2] // 2
    )

    def attend_block(running, shard_piece):
        peak_old, denom_old, accum_old = running
        key_block = shard_piece[..., :head_dim]
        value_block = shard_piece[..., head_dim:]
        scores = jnp.einsum(
            "skmd,snkd->sknm", query_wide, key_block, preferred_element_type=jnp.float32
        )
        key_pos = jnp.arange(shard_piece.shape[1])
        visible = key_pos[:, None] <= positions[None, :]
        masked = jnp.where(visible[None, None], scores, -jnp.inf)
        peak_new = jnp.maximum(peak_old, jnp.max(masked, axis=2))
        exp_terms = jnp.exp(masked - peak_new[:, :, None, :])
        factor = jnp.exp(peak_old - peak_new)
        denom_new = denom_old * factor + jnp.sum(exp_terms, axis=2)
        accum_new = accum_old * factor[:, :, None, :] + jnp.einsum(
            "sknm,snkd->skdm",
            exp_terms.astype(jnp.bfloat16),
            value_block,
            preferred_element_type=jnp.float32,
        )
        return (peak_new, denom_new, accum_new)

    shard_piece = lax.all_gather(keyvals, "ctx", axis=1, tiled=True)

    def keep_state(state_in):
        return state_in

    def update_state(state_in):
        return attend_block(state_in, shard_piece)

    peak_fin, denom_fin, accum_fin = lax.cond(
        jnp.int32(0) > last_pos, keep_state, update_state, start_state
    )
    normalized = (accum_fin / denom_fin[:, :, None, :]).reshape(
        local_seqs, kv_local, head_dim, query_group_size, tokens
    )
    attended = (
        jnp.transpose(normalized, (0, 4, 1, 3, 2))
        .reshape(row_count, q_local * head_dim)
        .astype(jnp.bfloat16)
    )
    partial_proj = jnp.dot(
        attended,
        lax.all_gather(out_weight, "ctx", axis=1, tiled=True),
        preferred_element_type=jnp.float32,
    )
    col_start = lax.axis_index("head") * col_width
    own_stream = stream.reshape(row_count, col_width).astype(jnp.float32)
    own_cols = lax.dynamic_slice_in_dim(partial_proj, col_start, col_width, 1) + own_stream
    placed = lax.dynamic_update_slice_in_dim(partial_proj, own_cols, col_start, 1)
    hidden_state = lax.psum(placed.astype(jnp.bfloat16), "head")
    state_float = hidden_state.astype(jnp.float32)
    inverse = lax.rsqrt(jnp.mean(state_float * state_float, axis=-1, keepdims=True) + 1e-05)
    send_rows = (state_float * inverse * norm_gain).astype(jnp.bfloat16)
    logits = jnp.dot(send_rows, router, preferred_element_type=jnp.float32)
    own_state = lax.dynamic_slice_in_dim(hidden_state, col_start, col_width, 1)
    expert_rows = expert_ids.reshape(row_count, expert_ids.shape[2])
    expert_count = router.shape[1]
    top_count = expert_rows.shape[1]
    member = expert_rows[:, :, None] == jnp.arange(expert_count)[None, None, :]
    chosen = jnp.sum(jnp.where(member, logits[:, None, :], 0.0), axis=-1)
    mix_weights = jax.nn.softmax(chosen, axis=-1)
    block_rows = row_count // rep_count
    member_int = member.astype(jnp.int32).reshape(rep_count, block_rows * top_count, expert_count)
    earlier = jnp.cumsum(member_int, axis=1) - member_int
    slot_rank = jnp.sum(earlier * member_int, axis=-1).reshape(row_count, top_count)
    target_rep = (jnp.arange(row_count) // block_rows)[:, None]
    local_halves = w_gate_up.shape[0]
    capacity = 3 * tokens // 16
    slot_total = ctx_count * rep_count * local_halves * capacity
    slot_lists = []
    for half_index in range(2):
        weight_row = 2 * expert_rows + half_index
        target_rank = weight_row // local_halves * rep_count + target_rep
        slot_lists.append(
            (target_rank * local_halves + weight_row % local_halves) * capacity + slot_rank
        )
    slot_index = jnp.stack(slot_lists, axis=-1)
    row_ids = jnp.broadcast_to(jnp.arange(row_count)[:, None, None], slot_index.shape)
    spread = (
        jnp.zeros((slot_total, row_count), jnp.bfloat16)
        .at[slot_index.reshape(-1), row_ids.reshape(-1)]
        .set(1.0)
    )
    outgoing = jnp.dot(spread, send_rows, preferred_element_type=jnp.float32).astype(jnp.bfloat16)
    outgoing = outgoing.reshape(ctx_count * rep_count, local_halves, capacity, send_rows.shape[1])
    gate_up = jnp.einsum(
        "sgcd,ghzd->sgczh",
        lax.all_to_all(outgoing, ("ctx", "rep"), split_axis=0, concat_axis=0, tiled=True),
        gate_up_weights,
        preferred_element_type=jnp.float32,
    )
    gate_part = gate_up[:, :, :, 0]
    up_part = gate_up[:, :, :, 1]
    active = (gate_part * jax.nn.sigmoid(1.702 * gate_part) * (up_part + 1.0)).astype(jnp.bfloat16)
    expert_out = jnp.einsum(
        "sgch,ghd->sgcd",
        lax.all_gather(active, "head", axis=3, tiled=True),
        w_down,
        preferred_element_type=jnp.float32,
    ).astype(jnp.bfloat16)
    returned = lax.all_to_all(expert_out, ("ctx", "rep"), split_axis=0, concat_axis=0, tiled=True)
    returned_rows = returned.reshape(slot_total, col_width)
    picked_rows = returned_rows[slot_index]
    combined = jnp.sum(mix_weights[:, :, None, None] * picked_rows.astype(jnp.float32), axis=(1, 2))
    layer_out = (own_state.astype(jnp.float32) + combined).astype(jnp.bfloat16)
    return layer_out.reshape(local_seqs, tokens, col_width)


def solution(mesh):
    placed = (
        P("rep", "ctx", "head"),
        P("rep", "ctx", "head", None),
        P("head"),
        P("rep", "ctx", "head"),
        P("head", "ctx"),
        P(),
        P(),
        P("rep", "ctx", None),
        P("ctx", "head", None),
        P("ctx", None, "head"),
    )
    return jax.shard_map(
        on_device, mesh=mesh, in_specs=placed, out_specs=P("rep", "ctx", "head"), check_vma=False
    )
```

profile of v0, /device:TPU:0, one launch (start us, length us, event | category | flops | bytes accessed | tf_op | source)
XLA Modules:
  0.0 661.9 jit_solution(3322971049654471776)
XLA Ops:
  6.5 0.7 all-gather.3.cloned.1.call-update
  7.3 0.8 copy.78
  8.1 0.1 eq.45
  8.2 0.1 eq.41
  8.3 0.7 broadcast_multiply_fusion.1
  9.1 0.8 copy.70
  9.9 1.2 reduce-window.6
  11.1 0.2 slice_reduce_fusion
  11.4 0.1 fusion.33
  11.5 0.1 reshape.724
  11.7 0.9 broadcast_multiply_fusion
  12.6 0.2 reshape.722
  12.8 16.1 %all_gather.9 = bf16[2,256,1,128]{3,0,2,1:T(2,128)(2,1)S(1)} all-gather(bf16[2,64,1,128]{3,0,2,1:T(2,128)(2,1)S(1)} %copy.70), channel_id=1, replica_groups=mesh['ctx'=4,'head'=4,'rep'=2] {'ctx'}, dimensions={1}, use_global_device_ids=true | all-gather | bytes 163840 | tf_op jit(solution)/shard_map/all_gather | solution.py:63
  28.9 2.4 conditional.1
  28.9 0.3 copy.72
  29.1 0.2 reshape.711
  29.4 0.7 broadcast_in_dim.35
  30.3 0.1 copy.71
  30.4 0.4 fusion.53
  30.8 0.2 fusion.2
  31.0 0.3 fusion
  31.3 0.2 convert_element_type.65
  31.5 0.3 copy.73
  31.8 0.2 convert_element_type.67
  32.1 0.2 copy.83
  32.2 0.3 reshape.725
  32.5 0.3 reshape.726
  32.9 0.2 copy.74
  33.0 39.7 %all-gather.3.cloned.1.call-done = bf16[512,2880]{0,1:T(8,128)(2,1)} async-done(((bf16[512,720]{0,1:T(8,128)(2,1)}), bf16[512,2880]{0,1:T(8,128)(2,1)}) %all-gather.3.cloned.1.call-update) | async-done | bytes 2949136 | tf_op jit(solution)/shard_map/all_gather | solution.py:84
  72.8 2.8 fusion.54
  75.6 0.9 convert_element_type.70
  76.8 8.2 %scatter_custom_fusion = bf16[196608]{0:T(1024)(128)(2,1)S(1)} fusion(s32[1024]{0:T(1024)S(1)} %broadcast_select_fusion, bf16[1024]{0:T(1024)(128)(2,1)S(1)} %broadcast.896, bf16[]{:T(256)} %constant.105.clone.1), kind=kCustom, calls=%fused_computation.44 | custom fusion | bytes 393218
  85.1 24.8 %all-reduce.2.cloned.1.call-done = bf16[128,2880]{0,1:T(8,128)(2,1)} async-done(((bf16[128,2880]{0,1:T(8,128)(2,1)}), bf16[128,2880]{0,1:T(8,128)(2,1)}) %all-reduce.2.cloned.1.call-update) | async-done | bytes 737296 | tf_op jit(solution)/shard_map/psum | solution.py:91
  109.9 1.5 fusion.22
  111.4 7.0 %convolution_convert_fusion = bf16[1536,2880]{0,1:T(8,128)(2,1)} fusion(bf16[196608]{0:T(1024)(128)(2,1)S(1)} %scatter_custom_fusion, bf16[128,2880]{0,1:T(8,128)(2,1)} %all-reduce.2.cloned.1.call-done, f32[2880]{0:T(1024)S(1)} %copy-done.4, f32[128]{0:T(128)S(1)} %add_rsqrt_fusion), kind=kOutput, calls=%fused_computation.24 | convolution fusion | flops 1138360320 | bytes 9989888 | tf_op jit(solution)/shard_map/dot_general | solution.py:125
  118.5 12.5 %copy.84 = bf16[1536,2880]{1,0:T(8,128)(2,1)} copy(bf16[1536,2880]{0,1:T(8,128)(2,1)} %convolution_convert_fusion) | data formatting | bytes 17694720 | tf_op jit(solution)/shard_map/convert_element_type | solution.py:125
  131.0 13.4 %reshape.727 = bf16[8,16,12,2880]{3,2,1,0:T(8,128)(2,1)} reshape(bf16[1536,2880]{1,0:T(8,128)(2,1)} %copy.84) | data formatting | bytes 17694720 | tf_op jit(solution)/shard_map/reshape | solution.py:126
  144.4 9.7 %copy.85 = bf16[8,16,12,2880]{3,1,2,0:T(8,128)(2,1)} copy(bf16[8,16,12,2880]{3,2,1,0:T(8,128)(2,1)} %reshape.727) | data formatting | bytes 17694720 | tf_op jit(solution)/shard_map/reshape | solution.py:126
  154.1 5.5 all-to-all-start
  159.7 55.8 %reshape.728 = bf16[16,180,2,2880]{3,2,0,1:T(2,128)(2,1)} reshape(bf16[16,180,5760]{2,0,1:T(8,128)(2,1)} %param.20) | data formatting | bytes 66355200 | tf_op jit(solution)/shard_map/reshape | solution.py:37
  215.5 140.7 %all-to-all-done = bf16[8,16,12,2880]{3,1,2,0:T(8,128)(2,1)} async-done(((bf16[8,16,12,2880]{3,1,2,0:T(8,128)(2,1)}), bf16[8,16,12,2880]{3,1,2,0:T(8,128)(2,1)}, u32[]{:S(2)}, u32[]{:S(2)}) %all-to-all-start) | async-done | bytes 8847392 | tf_op jit(solution)/shard_map/all_to_all | solution.py:129
  356.1 43.2 %fusion.14 = f32[8,16,12,2,180]{4,2,3,0,1:T(8,128)S(1)} fusion(bf16[16,180,2,2880,1]{3,2,0,1,4:T(2,128)(2,1)} %bitcast.104, bf16[8,16,12,2880,1]{3,1,2,0,4:T(8,128)(2,1)} %bitcast.12), kind=kOutput, calls=%fused_computation.27 | convolution fusion | flops 3185049600 | bytes 44236800 | tf_op jit(solution)/shard_map/sgcd,ghzd->sgczh/dot_general | solution.py:127
  399.3 1.6 fusion.21
  401.0 15.0 %copy.89 = bf16[8,16,12,180]{1,0,2,3:T(8,128)(2,1)} copy(bf16[8,16,12,180]{3,2,0,1:T(8,128)(2,1)} %fusion.21) | data formatting | bytes 1105920 | tf_op jit(solution)/shard_map/convert_element_type | solution.py:135
  416.0 112.2 %all-gather.5.cloned.1.call-done = bf16[8,16,12,720]{1,0,2,3:T(8,128)(2,1)} async-done(((bf16[8,16,12,180]{1,0,2,3:T(8,128)(2,1)}), bf16[8,16,12,720]{1,0,2,3:T(8,128)(2,1)}) %all-gather.5.cloned.1.call-update) | async-done | bytes 2211856 | tf_op jit(solution)/shard_map/all_gather | solution.py:138
  528.2 34.0 %copy.90 = bf16[8,16,12,720]{3,2,0,1:T(8,128)(2,1)S(1)} copy(bf16[8,16,12,720]{1,0,2,3:T(8,128)(2,1)} %all-gather.5.cloned.1.call-done) | data formatting | bytes 4423680 | tf_op jit(solution)/shard_map/all_gather | solution.py:138
  562.3 8.8 %convert_bitcast_fusion = bf16[8,16,12,720]{3,2,0,1:T(8,128)(2,1)S(1)} fusion(bf16[8,16,12,720]{3,2,0,1:T(8,128)(2,1)S(1)} %copy.90, bf16[16,720,720]{2,1,0:T(8,128)(2,1)} %param.21), kind=kOutput, calls=%fused_computation.26 | convolution fusion | flops 1593630720 | bytes 21012480 | tf_op jit(solution)/shard_map/sgch,ghd->sgcd/dot_general | solution.py:136
  571.0 2.7 copy.91
  573.8 5.9 all-to-all-start.1
  579.7 0.7 eq.37
  580.3 0.2 copy.93
  580.5 0.2 reshape.738
  580.8 1.3 fusion.27
  582.1 0.7 select_reduce_fusion
  582.8 0.1 copy.76
  583.0 50.9 %all-to-all-done.1 = bf16[8,16,12,720]{3,1,2,0:T(8,128)(2,1)S(1)} async-done(((bf16[8,16,12,720]{3,1,2,0:T(8,128)(2,1)}), bf16[8,16,12,720]{3,1,2,0:T(8,128)(2,1)S(1)}, u32[]{:S(2)}, u32[]{:S(2)}) %all-to-all-start.1) | async-done | bytes 2211872 | tf_op jit(solution)/shard_map/all_to_all | solution.py:142
  633.9 2.6 copy.92
  636.4 4.0 reshape.729
  640.4 5.2 gather_fusion
  645.7 3.5 reshape.751
  649.2 3.0 multiply_reduce_fusion
  652.1 1.2 copy.94
  653.3 1.0 add_convert_fusion
  654.3 0.8 copy.95
  (53 shorter events, 1.1 us)
Async XLA Ops:
  6.5 574.2 %copy-start = (bf16[2880,32]{0,1:T(8,128)(2,1)S(1)}, bf16[2880,32]{0,1:T(8,128)(2,1)}, u32[]{:S(2)}) copy-start(bf16[2880,32]{0,1:T(8,128)(2,1)} %param.18) | copy-start | bytes 552964
  6.5 66.2 %all-gather.3.cloned.1.call-start = ((), (), s32[]{:S(2)}) async-start(), calls=%async_computation.2 | async-start | bytes 3686400 | tf_op jit(solution)/shard_map/all_gather | solution.py:84
  7.3 102.7 %all-reduce.2.cloned.1.call-start = ((), (), s32[]{:S(2)}) async-start(), calls=%async_computation.3 | async-start | bytes 1474560 | tf_op jit(solution)/shard_map/psum | solution.py:91
  28.9 3.9 copy-start.2
  75.5 1.1 copy-start.7
  75.5 1.2 copy-start.6
  75.6 35.9 %copy-start.4 = (f32[2880]{0:T(1024)S(1)}, f32[2880]{0:T(1024)}, u32[]{:S(2)}) copy-start(f32[2880]{0:T(1024)} %param.17) | copy-start | bytes 34564
  111.4 7.1 %copy-start.5 = (f32[128]{0:T(128)}, f32[128]{0:T(128)S(1)}, u32[]{:S(2)}) copy-start(f32[128]{0:T(128)S(1)} %add_rsqrt_fusion) | copy-start | bytes 1540
  154.1 202.0 %all-to-all-start = ((bf16[8,16,12,2880]{3,1,2,0:T(8,128)(2,1)}), bf16[8,16,12,2880]{3,1,2,0:T(8,128)(2,1)}, u32[]{:S(2)}, u32[]{:S(2)}) async-start(bf16[8,16,12,2880]{3,1,2,0:T(8,128)(2,1)} %copy.85), calls=%async_computation | async-start | bytes 18087936 | tf_op jit(solution)/shard_map/all_to_all | solution.py:129
  159.7 368.6 %all-gather.5.cloned.1.call-start = ((), (), s32[]{:S(2)}) async-start(), calls=%async_computation.4 | async-start | bytes 22118400 | tf_op jit(solution)/shard_map/all_gather | solution.py:138
  573.8 5.9 copy-start.3
  573.8 7.0 %copy-start.1 = (bf16[128,2880]{0,1:T(8,128)(2,1)S(1)}, bf16[128,2880]{0,1:T(8,128)(2,1)}, u32[]{:S(2)}) copy-start(bf16[128,2880]{0,1:T(8,128)(2,1)} %all-reduce.2.cloned.1.call-done) | copy-start | bytes 2211844
  573.8 60.1 %all-to-all-start.1 = ((bf16[8,16,12,720]{3,1,2,0:T(8,128)(2,1)}), bf16[8,16,12,720]{3,1,2,0:T(8,128)(2,1)S(1)}, u32[]{:S(2)}, u32[]{:S(2)}) async-start(bf16[8,16,12,720]{3,1,2,0:T(8,128)(2,1)} %copy.91), calls=%async_computation.1 | async-start | bytes 4718592 | tf_op jit(solution)/shard_map/all_to_all | solution.py:142
Sparse Core Ops, SparseCore 0:
  8.9 63.8 all-gather.2
  76.7 33.1 all-reduce.1
  416.1 112.0 all-gather.4
where the time goes:
time: 671 us; the launch traced here: 662 us
  waiting for transfers between devices  369 us (55%)
  local copies, waits for them, and re-layouts  175 us (26%)
  matrix products  63.7 us (9%)
  blocking collectives  16.1 us (2%)
  between operations  13.7 us (2%)
  other arithmetic  12.4 us (2%)
  starting transfers between devices  11.5 us (2%)
    all_to_all x1, waiting for transfers between devices, on_device(): lax.all_to_all(outgoing, ('ctx', 'rep'), split_axis=0, concat_axis=0, til...  141 us
    all_gather x1, waiting for transfers between devices, on_device(): lax.all_gather(active, 'head', axis=3, tiled=True)  112 us
    reshape x1, local copies, waits for them, and re-layouts, on_device(): w_gate_up.reshape(w_gate_up.shape[0], w_gate_up.shape[1], 2, w_gate_up.sh...  55.8 us
    all_to_all x1, waiting for transfers between devices, on_device(): lax.all_to_all(expert_out, ('ctx', 'rep'), split_axis=0, concat_axis=0, t...  50.9 us
    dot_general x1, matrix products, on_device(): jnp.einsum('sgcd,ghzd->sgczh', lax.all_to_all(outgoing, ('ctx', 'rep'), s...  43.2 us
    all_gather x1, waiting for transfers between devices, on_device(): lax.all_gather(out_weight, 'ctx', axis=1, tiled=True)  39.7 us
    all_gather x1, local copies, waits for them, and re-layouts, on_device(): lax.all_gather(active, 'head', axis=3, tiled=True)  34 us
    psum x1, waiting for transfers between devices, on_device(): hidden_state = lax.psum(placed.astype(jnp.bfloat16), 'head')  24.8 us
  transfers between devices with their start and end apart: 5, of which 5 were waited for; matrix products, arithmetic and copies ran while one was open for 12% of the time, Pallas kernels for 0%

commit v1 on v0

--- a/solution.py
+++ b/solution.py
@@ -2,6 +2,12 @@
 import jax.numpy as jnp
 from jax import lax
 from jax.sharding import PartitionSpec as P
+
+
+def gather_by_exchange(x, axis, dim):
+    count = lax.axis_size(axis)
+    repeats = [count if d == dim else 1 for d in range(x.ndim)]
+    return lax.all_to_all(jnp.tile(x, repeats), axis, split_axis=dim, concat_axis=dim, tiled=True)
 
 
 def on_device(
@@ -80,9 +86,7 @@
         .astype(jnp.bfloat16)
     )
     partial_proj = jnp.dot(
-        attended,
-        lax.all_gather(out_weight, "ctx", axis=1, tiled=True),
-        preferred_element_type=jnp.float32,
+        attended, gather_by_exchange(out_weight, "ctx", 1), preferred_element_type=jnp.float32
     )
     col_start = lax.axis_index("head") * col_width
     own_stream = stream.reshape(row_count, col_width).astype(jnp.float32)

time: 671 us -> 701 us (1.045)
  blocking collectives: 16.1 us -> 69.8 us
  waiting for transfers between devices: 369 us -> 330 us
  local copies, waits for them, and re-layouts: 175 us -> 183 us
    all_gather x1, blocking collectives: 16.1 us -> 69.8 us  [on_device(): shard_piece = lax.all_gather(keyvals, 'ctx', axis=1, tiled=True)]
    all_gather x1 -> x0, waiting for transfers between devices: 39.7 us -> none  [on_device(): lax.all_gather(out_weight, 'ctx', axis=1, tiled=True)]
  transfers between devices with their start and end apart: 5 -> 5, of which waited for: 5 -> 4; matrix products, arithmetic and copies ran while one was open for 12% -> 12% of each run, Pallas kernels for 0% -> 0%
where the time goes in v1:
time: 701 us; the launch traced here: 691 us
  waiting for transfers between devices  330 us (47%)
  local copies, waits for them, and re-layouts  183 us (26%)
  blocking collectives  69.8 us (10%)
  matrix products  64.5 us (9%)
  starting transfers between devices  17.9 us (3%)
  between operations  14 us (2%)
  other arithmetic  11.7 us (2%)
    all_to_all x1, waiting for transfers between devices, on_device(): lax.all_to_all(outgoing, ('ctx', 'rep'), split_axis=0, concat_axis=0, til...  141 us
    all_gather x1, waiting for transfers between devices, on_device(): lax.all_gather(active, 'head', axis=3, tiled=True)  112 us
    all_gather x1, blocking collectives, on_device(): shard_piece = lax.all_gather(keyvals, 'ctx', axis=1, tiled=True)  69.8 us
    reshape x1, local copies, waits for them, and re-layouts, on_device(): w_gate_up.reshape(w_gate_up.shape[0], w_gate_up.shape[1], 2, w_gate_up.sh...  55.8 us
    all_to_all x1, waiting for transfers between devices, on_device(): lax.all_to_all(expert_out, ('ctx', 'rep'), split_axis=0, concat_axis=0, t...  50.9 us
    dot_general x1, matrix products, on_device(): jnp.einsum('sgcd,ghzd->sgczh', lax.all_to_all(outgoing, ('ctx', 'rep'), s...  43.2 us
    all_gather x1, local copies, waits for them, and re-layouts, on_device(): lax.all_gather(active, 'head', axis=3, tiled=True)  34 us
    psum x1, waiting for transfers between devices, on_device(): hidden_state = lax.psum(placed.astype(jnp.bfloat16), 'head')  26.4 us
  transfers between devices with their start and end apart: 5, of which 4 were waited for; matrix products, arithmetic and copies ran while one was open for 12% of the time, Pallas kernels for 0%

profile of v1, /device:TPU:0, one launch (start us, length us, event | category | flops | bytes accessed | tf_op | source)
XLA Modules:
  0.0 691.1 jit_solution(13125044908126208703)
XLA Ops:
  6.5 3.0 tile.6
  9.5 6.5 all-to-all-start
  16.0 0.1 copy.79
  16.1 0.1 eq.45
  16.2 0.1 eq.41
  16.5 0.6 copy.71
  17.1 1.2 reduce-window.6
  18.3 0.2 slice_reduce_fusion
  18.6 0.1 fusion.33
  18.7 0.1 reshape.731
  18.9 0.2 reshape.729
  19.1 69.8 %all_gather.6 = bf16[2,256,1,128]{3,0,2,1:T(2,128)(2,1)S(1)} all-gather(bf16[2,64,1,128]{3,0,2,1:T(2,128)(2,1)} %copy.71), channel_id=1, replica_groups=mesh['ctx'=4,'head'=4,'rep'=2] {'ctx'}, dimensions={1}, use_global_device_ids=true | all-gather | bytes 163840 | tf_op jit(solution)/shard_map/all_gather | solution.py:69
  88.8 6.4 conditional.1
  88.8 1.0 copy.73
  89.8 1.2 reshape.718
  91.1 0.7 broadcast_in_dim.35
  91.9 0.8 copy.72
  92.7 1.2 fusion.53
  93.9 0.2 fusion.2
  94.1 1.1 fusion
  95.3 0.2 convert_element_type.65
  95.5 1.0 copy.74
  96.5 1.8 convert_element_type.67
  98.3 0.2 copy.84
  98.5 0.3 reshape.732
  98.8 0.3 reshape.733
  99.1 1.0 bitcast_convert_fusion
  100.0 0.9 copy.75
  101.0 1.9 fusion.54
  103.0 0.9 convert_element_type.70
  104.0 0.1 and_reduce_fusion
  104.2 8.2 %scatter_custom_fusion = bf16[196608]{0:T(1024)(128)(2,1)S(1)} fusion(s32[1024]{0:T(1024)S(1)} %broadcast_select_fusion, bf16[1024]{0:T(1024)(128)(2,1)S(1)} %broadcast.899, bf16[]{:T(256)} %constant.105.clone.1), kind=kCustom, calls=%fused_computation.44 | custom fusion | bytes 393218
  112.4 26.4 %all-reduce.2.cloned.1.call-done = bf16[128,2880]{0,1:T(8,128)(2,1)} async-done(((bf16[128,2880]{0,1:T(8,128)(2,1)}), bf16[128,2880]{0,1:T(8,128)(2,1)}) %all-reduce.2.cloned.1.call-update) | async-done | bytes 737296 | tf_op jit(solution)/shard_map/psum | solution.py:95
  138.8 1.5 fusion.22
  140.3 7.0 %convolution_convert_fusion = bf16[1536,2880]{0,1:T(8,128)(2,1)} fusion(bf16[196608]{0:T(1024)(128)(2,1)S(1)} %scatter_custom_fusion, bf16[128,2880]{0,1:T(8,128)(2,1)} %all-reduce.2.cloned.1.call-done, f32[2880]{0:T(1024)S(1)} %copy-done.6, f32[128]{0:T(128)S(1)} %add_rsqrt_fusion), kind=kOutput, calls=%fused_computation.24 | convolution fusion | flops 1138360320 | bytes 9989888 | tf_op jit(solution)/shard_map/dot_general | solution.py:129
  147.4 12.5 %copy.85 = bf16[1536,2880]{1,0:T(8,128)(2,1)} copy(bf16[1536,2880]{0,1:T(8,128)(2,1)} %convolution_convert_fusion) | data formatting | bytes 17694720 | tf_op jit(solution)/shard_map/convert_element_type | solution.py:129
  159.8 13.4 %reshape.734 = bf16[8,16,12,2880]{3,2,1,0:T(8,128)(2,1)} reshape(bf16[1536,2880]{1,0:T(8,128)(2,1)} %copy.85) | data formatting | bytes 17694720 | tf_op jit(solution)/shard_map/reshape | solution.py:130
  173.3 9.7 %copy.86 = bf16[8,16,12,2880]{3,1,2,0:T(8,128)(2,1)} copy(bf16[8,16,12,2880]{3,2,1,0:T(8,128)(2,1)} %reshape.734) | data formatting | bytes 17694720 | tf_op jit(solution)/shard_map/reshape | solution.py:130
  183.0 5.5 all-to-all-start.1
  188.6 55.8 %reshape.735 = bf16[16,180,2,2880]{3,2,0,1:T(2,128)(2,1)} reshape(bf16[16,180,5760]{2,0,1:T(8,128)(2,1)} %param.20) | data formatting | bytes 66355200 | tf_op jit(solution)/shard_map/reshape | solution.py:43
  244.4 140.7 %all-to-all-done.1 = bf16[8,16,12,2880]{3,1,2,0:T(8,128)(2,1)} async-done(((bf16[8,16,12,2880]{3,1,2,0:T(8,128)(2,1)}), bf16[8,16,12,2880]{3,1,2,0:T(8,128)(2,1)}, u32[]{:S(2)}, u32[]{:S(2)}) %all-to-all-start.1) | async-done | bytes 8847392 | tf_op jit(solution)/shard_map/all_to_all | solution.py:133
  385.0 43.2 %fusion.14 = f32[8,16,12,2,180]{4,2,3,0,1:T(8,128)S(1)} fusion(bf16[16,180,2,2880,1]{3,2,0,1,4:T(2,128)(2,1)} %bitcast.105, bf16[8,16,12,2880,1]{3,1,2,0,4:T(8,128)(2,1)} %bitcast.13), kind=kOutput, calls=%fused_computation.27 | convolution fusion | flops 3185049600 | bytes 44236800 | tf_op jit(solution)/shard_map/sgcd,ghzd->sgczh/dot_general | solution.py:131
  428.2 1.6 fusion.21
  429.9 15.0 %copy.90 = bf16[8,16,12,180]{1,0,2,3:T(8,128)(2,1)} copy(bf16[8,16,12,180]{3,2,0,1:T(8,128)(2,1)} %fusion.21) | data formatting | bytes 1105920 | tf_op jit(solution)/shard_map/convert_element_type | solution.py:139
  444.9 112.2 %all-gather.2.cloned.1.call-done = bf16[8,16,12,720]{1,0,2,3:T(8,128)(2,1)} async-done(((bf16[8,16,12,180]{1,0,2,3:T(8,128)(2,1)}), bf16[8,16,12,720]{1,0,2,3:T(8,128)(2,1)}) %all-gather.2.cloned.1.call-update) | async-done | bytes 2211856 | tf_op jit(solution)/shard_map/all_gather | solution.py:142
  557.1 34.0 %copy.91 = bf16[8,16,12,720]{3,2,0,1:T(8,128)(2,1)S(1)} copy(bf16[8,16,12,720]{1,0,2,3:T(8,128)(2,1)} %all-gather.2.cloned.1.call-done) | data formatting | bytes 4423680 | tf_op jit(solution)/shard_map/all_gather | solution.py:142
  591.1 8.8 %convert_bitcast_fusion = bf16[8,16,12,720]{3,2,0,1:T(8,128)(2,1)S(1)} fusion(bf16[8,16,12,720]{3,2,0,1:T(8,128)(2,1)S(1)} %copy.91, bf16[16,720,720]{2,1,0:T(8,128)(2,1)} %param.21), kind=kOutput, calls=%fused_computation.26 | convolution fusion | flops 1593630720 | bytes 21012480 | tf_op jit(solution)/shard_map/sgch,ghd->sgcd/dot_general | solution.py:140
  599.9 2.7 copy.92
  602.7 5.9 all-to-all-start.2
  608.6 0.7 eq.37
  609.2 0.2 copy.94
  609.4 0.2 reshape.745
  609.7 1.3 fusion.27
  611.0 0.7 select_reduce_fusion
  611.7 0.1 copy.77
  611.8 50.9 %all-to-all-done.2 = bf16[8,16,12,720]{3,1,2,0:T(8,128)(2,1)S(1)} async-done(((bf16[8,16,12,720]{3,1,2,0:T(8,128)(2,1)}), bf16[8,16,12,720]{3,1,2,0:T(8,128)(2,1)S(1)}, u32[]{:S(2)}, u32[]{:S(2)}) %all-to-all-start.2) | async-done | bytes 2211872 | tf_op jit(solution)/shard_map/all_to_all | solution.py:146
  662.8 2.6 copy.93
  665.3 4.0 reshape.736
  669.3 5.2 gather_fusion
  674.5 3.5 reshape.758
  678.1 3.0 multiply_reduce_fusion
  681.0 1.2 copy.95
  682.2 1.0 add_convert_fusion
  683.2 0.8 copy.96
  (57 shorter events, 1.0 us)
Async XLA Ops:
  6.5 603.1 %copy-start = (bf16[2880,32]{0,1:T(8,128)(2,1)S(1)}, bf16[2880,32]{0,1:T(8,128)(2,1)}, u32[]{:S(2)}) copy-start(bf16[2880,32]{0,1:T(8,128)(2,1)} %param.18) | copy-start | bytes 552964
  9.5 6.5 copy-start.4
  9.5 6.9 %copy-start.5 = (bf16[2,64,1,128]{3,1,2,0:T(8,128)(2,1)S(1)}, bf16[2,64,1,128]{3,1,2,0:T(8,128)(2,1)}, u32[]{:S(2)}) copy-start(bf16[2,64,1,128]{3,1,2,0:T(8,128)(2,1)} %param.13) | copy-start | bytes 98308
  9.5 9.3 %copy-start.3 = (bf16[2,64,512]{2,1,0:T(8,128)(2,1)S(1)}, bf16[2,64,512]{2,1,0:T(8,128)(2,1)}, u32[]{:S(2)}) copy-start(bf16[2,64,512]{2,1,0:T(8,128)(2,1)} %param.12) | copy-start | bytes 393220
  9.5 91.4 %all-to-all-start = ((bf16[512,4,720]{0,2,1:T(8,128)(2,1)}), bf16[512,4,720]{0,2,1:T(8,128)(2,1)S(1)}, u32[]{:S(2)}, u32[]{:S(2)}) async-start(bf16[512,4,720]{0,2,1:T(8,128)(2,1)} %tile.6), calls=%async_computation | async-start | bytes 5898240 | tf_op jit(solution)/shard_map/all_to_all | solution.py:10
  16.0 122.8 %all-reduce.2.cloned.1.call-start = ((), (), s32[]{:S(2)}) async-start(), calls=%async_computation.3 | async-start | bytes 1474560 | tf_op jit(solution)/shard_map/psum | solution.py:95
  101.0 1.9 copy-start.2
  102.9 1.1 copy-start.9
  102.9 1.2 copy-start.8
  102.9 37.4 %copy-start.6 = (f32[2880]{0:T(1024)S(1)}, f32[2880]{0:T(1024)}, u32[]{:S(2)}) copy-start(f32[2880]{0:T(1024)} %param.17) | copy-start | bytes 34564
  140.3 7.1 %copy-start.7 = (f32[128]{0:T(128)}, f32[128]{0:T(128)S(1)}, u32[]{:S(2)}) copy-start(f32[128]{0:T(128)S(1)} %add_rsqrt_fusion) | copy-start | bytes 1540
  183.0 202.0 %all-to-all-start.1 = ((bf16[8,16,12,2880]{3,1,2,0:T(8,128)(2,1)}), bf16[8,16,12,2880]{3,1,2,0:T(8,128)(2,1)}, u32[]{:S(2)}, u32[]{:S(2)}) async-start(bf16[8,16,12,2880]{3,1,2,0:T(8,128)(2,1)} %copy.86), calls=%async_computation.1 | async-start | bytes 18087936 | tf_op jit(solution)/shard_map/all_to_all | solution.py:133
  188.6 368.6 %all-gather.2.cloned.1.call-start = ((), (), s32[]{:S(2)}) async-start(), calls=%async_computation.4 | async-start | bytes 22118400 | tf_op jit(solution)/shard_map/all_gather | solution.py:142
  602.7 7.0 %copy-start.1 = (bf16[128,2880]{0,1:T(8,128)(2,1)S(1)}, bf16[128,2880]{0,1:T(8,128)(2,1)}, u32[]{:S(2)}) copy-start(bf16[128,2880]{0,1:T(8,128)(2,1)} %all-reduce.2.cloned.1.call-done) | copy-start | bytes 2211844
  602.7 60.1 %all-to-all-start.2 = ((bf16[8,16,12,720]{3,1,2,0:T(8,128)(2,1)}), bf16[8,16,12,720]{3,1,2,0:T(8,128)(2,1)S(1)}, u32[]{:S(2)}, u32[]{:S(2)}) async-start(bf16[8,16,12,720]{3,1,2,0:T(8,128)(2,1)} %copy.92), calls=%async_computation.2 | async-start | bytes 4718592 | tf_op jit(solution)/shard_map/all_to_all | solution.py:146
Sparse Core Ops, SparseCore 0:
  104.1 34.6 all-reduce.1
  445.0 112.0 all-gather.1
